TPU v7x, 128 devices: a whole 4x4x4 slice. The times are simulated.
128 devices in a mesh: seq: 4 (over x), tp: 32 (over z, y, core).
Axes of the slice: x: 4, y: 4, z: 4, core: 2. Of those that a mesh axis runs over, the one named last changes fastest.
Arguments:
- hidden_in: bfloat16 [96, 4, 1024], P('tp'), may hold values from -6 to 6
- new_query: bfloat16 [96, 4, 1024], P('tp'), may hold values from -70 to 70
- new_key: bfloat16 [96, 4, 1024], P('tp'), may hold values from -15 to 15
- new_value: bfloat16 [96, 4, 1024], P('tp'), may hold values from -6 to 6
- key_cache: bfloat16 [96, 4096, 1024], P('tp', 'seq'), may hold values from -16 to 16
- value_cache: bfloat16 [96, 4096, 1024], P('tp', 'seq'), may hold values from -6 to 6
- lengths: int32 [96], P('tp'), may hold values from 64 to 4096, as said below
- out_weight: bfloat16 [1024, 1024], replicated, may hold values from -0.1875 to 0.1875
- norm_gain: float32 [1024], replicated, may hold values from 0.5 to 1.5
- router_weight: bfloat16 [1024, 16], replicated, may hold values from -0.1875 to 0.1875
- expert_ids: int32 [96, 4, 2], P('tp'), may hold values from 0 to 15, all different within a row
- gate_weight: bfloat16 [45056, 1024], P(('seq', 'tp')), may hold values from -0.1875 to 0.1875
- up_weight: bfloat16 [45056, 1024], P(('seq', 'tp')), may hold values from -0.1875 to 0.1875
- down_weight: bfloat16 [45056, 1024], P(('seq', 'tp')), may hold values from -0.109375 to 0.109375
Outputs:
- attn_out: bfloat16 [96, 4, 1024], P('tp', None, 'seq')
- layer_out: bfloat16 [96, 4, 1024], P('tp', None, 'seq')
Inputs may be any that keep to these rules, and one draw needn't show every extreme that they name: `lengths`: each length is 4096 or between 64 and 128; some request has 4096.
All inputs are finite; a program needn't handle non-finite values.
Results may differ from a plain program's by a relative error of at most 0.014.
Values may be sent and summed in bfloat16 or wider, within the bound.
A program may use at most 64 MiB of HBM per device.

v0:
```python
import jax
import jax.numpy as jnp
from jax import lax
from jax.sharding import PartitionSpec as P

HEADS = 16
masked_score = -1e30
norm_epsilon = 1e-06


def entering(part, axis, combine, identity):
    place = lax.axis_index(axis)
    gathered = lax.all_gather(part, axis)
    state = jnp.zeros_like(part) + jnp.asarray(identity, part.dtype)

    def one(turn, state):
        return combine(state, lax.dynamic_index_in_dim(gathered, turn, 0, False))

    return lax.fori_loop(0, place, one, state)


def add_counts(former, latter):
    return former + latter


def pick_slot(chosen_ids, earlier):
    onehot = chosen_ids[..., None] == jnp.arange(earlier.shape[2], dtype=jnp.int32)
    return jnp.sum(jnp.where(onehot, earlier[:, :, None, :], 0), axis=3)


def body(
    hidden_in,
    new_query,
    new_key,
    new_value,
    key_cache,
    value_cache,
    lengths,
    out_weight,
    norm_gain,
    router_weight,
    expert_ids,
    gate_weight,
    up_weight,
    down_weight,
):
    req_dev, steps, width = hidden_in.shape
    block = key_cache.shape[1]
    head_size = width // HEADS
    scale = head_size ** (-0.5)
    seq_index = lax.axis_index("seq")
    tp_index = lax.axis_index("tp")
    seq_size = lax.axis_size("seq")
    tp_size = lax.axis_size("tp")
    queries = new_query.reshape(req_dev, steps, HEADS, head_size)
    cache_keys = key_cache.reshape(req_dev, block, HEADS, head_size)
    cache_values = value_cache.reshape(req_dev, block, HEADS, head_size)
    fresh_keys = new_key.reshape(req_dev, steps, HEADS, head_size)
    fresh_values = new_value.reshape(req_dev, steps, HEADS, head_size)
    scores = (
        jnp.einsum("rthe,rphe->rhtp", queries, cache_keys, preferred_element_type=jnp.float32)
        * scale
    )
    positions = seq_index * block + jnp.arange(block, dtype=jnp.int32)
    usable = (positions[None, :] < lengths[:, None])[:, None, None, :]
    scores = jnp.where(usable, scores, masked_score)
    fresh_scores = (
        jnp.einsum("rthe,rshe->rhts", queries, fresh_keys, preferred_element_type=jnp.float32)
        * scale
    )
    causal = (jnp.arange(steps)[:, None] >= jnp.arange(steps)[None, :]) & (seq_index == 0)
    fresh_scores = jnp.where(causal, fresh_scores, masked_score)
    local_max = jnp.maximum(jnp.max(scores, axis=3), jnp.max(fresh_scores, axis=3))
    weights = jnp.where(usable, jnp.exp(scores - local_max[..., None]), 0.0)
    fresh_weights = jnp.where(causal, jnp.exp(fresh_scores - local_max[..., None]), 0.0)
    totals = jnp.sum(weights, axis=3) + jnp.sum(fresh_weights, axis=3)
    gathered_values = jnp.einsum(
        "rhtp,rphe->rhte",
        weights.astype(jnp.bfloat16),
        cache_values,
        preferred_element_type=jnp.float32,
    )
    gathered_values = gathered_values + jnp.einsum(
        "rhts,rshe->rhte",
        fresh_weights.astype(jnp.bfloat16),
        fresh_values,
        preferred_element_type=jnp.float32,
    )
    overall = lax.pmax(local_max, "seq")
    factors = jnp.exp(local_max - overall)
    totals, gathered_values = (
        lax.psum((totals * factors).astype(jnp.bfloat16), "seq").astype(jnp.float32),
        lax.psum((gathered_values * factors[..., None]).astype(jnp.bfloat16), "seq").astype(
            jnp.float32
        ),
    )
    context = (
        (gathered_values / totals[..., None])
        .transpose(0, 2, 1, 3)
        .reshape(req_dev, steps, width)
        .astype(jnp.bfloat16)
    )
    attention = jnp.einsum("rtd,de->rte", context, out_weight, preferred_element_type=jnp.float32)
    feature_block = width // seq_size
    attn_out = lax.dynamic_slice_in_dim(
        attention, seq_index * feature_block, feature_block, 2
    ).astype(jnp.bfloat16)
    residual = hidden_in.astype(jnp.float32) + attention
    normed = (
        residual
        * lax.rsqrt(jnp.mean(residual * residual, axis=-1, keepdims=True) + norm_epsilon)
        * norm_gain
    ).astype(jnp.bfloat16)
    experts = router_weight.shape[1]
    topk = expert_ids.shape[2]
    requests = req_dev * tp_size
    capacity = (5 * requests * topk + 4 * experts - 1) // (4 * experts)
    expert_range = jnp.arange(experts, dtype=jnp.int32)
    local_hits = jnp.sum((expert_ids[..., None] == expert_range).astype(jnp.int32), axis=2)
    counts = jnp.sum(local_hits, axis=0)
    before = entering(counts, "tp", add_counts, jnp.zeros_like(counts))
    earlier = (before[None] + jnp.cumsum(local_hits, axis=0) - local_hits).astype(jnp.int32)
    routing = jnp.concatenate([expert_ids, pick_slot(expert_ids, earlier)], axis=2)
    all_routing = lax.all_gather(routing, "tp", axis=0, tiled=True)
    all_ids = all_routing[:, :, :topk]
    all_slots = all_routing[:, :, topk:]
    all_normed = lax.all_gather(normed, "tp", axis=0, tiled=True)
    logits = jnp.einsum(
        "rtd,de->rte", all_normed, router_weight, preferred_element_type=jnp.float32
    )
    onehot = all_ids[..., None] == expert_range
    chosen = jnp.sum(jnp.where(onehot, logits[:, :, None, :], 0.0), axis=3)
    share = 1.0 / (1.0 + jnp.exp(chosen[:, :, ::-1] - chosen))
    slices = seq_size * tp_size // experts
    mine = (seq_index * tp_size + tp_index) // slices
    match = all_ids == mine
    slot_mine = jnp.sum(jnp.where(match, all_slots, 0), axis=2)
    share_mine = jnp.sum(jnp.where(match, share, 0.0), axis=2)
    kept = jnp.any(match, axis=2) & (slot_mine < capacity)
    select = kept[None] & (slot_mine[None] == jnp.arange(capacity, dtype=jnp.int32)[:, None, None])
    buffer = (
        jnp.einsum(
            "crt,rtd->tcd",
            select.astype(jnp.bfloat16),
            all_normed,
            preferred_element_type=jnp.float32,
        )
        .astype(jnp.bfloat16)
        .reshape(steps * capacity, width)
    )
    contract = (((1,), (1,)), ((), ()))
    gate = lax.dot_general(buffer, gate_weight, contract, preferred_element_type=jnp.float32)
    upward = lax.dot_general(buffer, up_weight, contract, preferred_element_type=jnp.float32)
    inner = (jax.nn.gelu(gate) * upward).astype(jnp.bfloat16)
    produced = jnp.dot(inner, down_weight, preferred_element_type=jnp.float32)
    placed = select.astype(jnp.float32) * share_mine[None]
    term = jnp.einsum(
        "crt,tcd->rtd",
        placed,
        produced.reshape(steps, capacity, width),
        precision=lax.Precision.HIGHEST,
    )
    row_sums = lax.psum_scatter(term.astype(jnp.bfloat16), "tp", scatter_dimension=0, tiled=True)
    mixture = lax.psum_scatter(row_sums, "seq", scatter_dimension=2, tiled=True).astype(jnp.float32)
    own_residual = lax.dynamic_slice_in_dim(residual, seq_index * feature_block, feature_block, 2)
    layer_out = (own_residual + mixture).astype(jnp.bfloat16)
    return (attn_out, layer_out)


def solution(mesh):
    return jax.shard_map(
        body,
        mesh=mesh,
        in_specs=(
            P("tp", None, None),
            P("tp", None, None),
            P("tp", None, None),
            P("tp", None, None),
            P("tp", "seq", None),
            P("tp", "seq", None),
            P("tp"),
            P(),
            P(),
            P(),
            P("tp", None, None),
            P(("seq", "tp"), None),
            P(("seq", "tp"), None),
            P(("seq", "tp"), None),
        ),
        out_specs=(P("tp", None, "seq"), P("tp", None, "seq")),
        check_vma=False,
    )
```

profile of v0, /device:TPU:0, one launch (start us, length us, event | category | flops | bytes accessed | tf_op | source)
XLA Modules:
  0.0 284.9 jit_solution(4095929092177931425)
XLA Ops:
  7.2 1.0 reshape.92
  8.2 8.7 %copy.131 = bf16[3,1024,1024]{1,2,0:T(8,128)(2,1)} copy(bf16[3,1024,1024]{2,1,0:T(8,128)(2,1)} %param.20) | data formatting | bytes 12582912 | tf_op args[4]
  17.0 0.2 fusion.30
  17.6 3.8 %fusion.61 = (f32[3,16,4]{2,1,0:T(8,128)S(1)}, f32[3,16,4,1024]{3,2,1,0:T(4,128)S(1)}) fusion(bf16[3,1024,16,64]{1,3,2,0:T(8,128)(2,1)} %bitcast.35, bf16[3,4,16,64]{3,2,1,0:T(8,128)(2,1)S(1)} %reshape.92, pred[3,1024]{1,0:T(4,128)(4,1)S(1)} %broadcast_compare_fusion), kind=kOutput, calls=%fused_computation.93 | convolution fusion | flops 25755456 | bytes 7106304 | tf_op jit(solution)/shard_map/rthe,rphe->rhtp/dot_general | solution.py:61
  21.5 17.1 %pmax.7 = f32[3,16,4]{2,1,0:T(8,128)S(1)} all-reduce(f32[3,16,4]{2,1,0:T(8,128)S(1)} %max.9), channel_id=1, replica_groups=mesh['seq'=4,'tp'=32] {'seq'}, use_global_device_ids=true, to_apply=%region_2.3 | all-reduce | flops 192 | bytes 1536 | tf_op jit(solution)/shard_map/pmax | solution.py:89
  38.6 0.5 fusion.12
  39.3 8.6 %copy.137 = bf16[3,1024,1024]{1,2,0:T(8,128)(2,1)} copy(bf16[3,1024,1024]{2,1,0:T(8,128)(2,1)} %param.21) | data formatting | bytes 12582912 | tf_op args[5]
  48.0 4.6 %fusion.14 = f32[3,16,4,64]{3,2,1,0:T(4,128)S(1)} fusion(bf16[3,1024,16,64]{1,3,2,0:T(8,128)(2,1)} %bitcast.36, f32[3,16,4,1024]{3,2,1,0:T(4,128)S(1)} %get-tuple-element.49, f32[3,16,4]{2,1,0:T(8,128)S(1)} %max.9, pred[3,1024]{1,0:T(4,128)(4,1)S(1)} %broadcast_compare_fusion), kind=kOutput, calls=%fused_computation.22 | convolution fusion | flops 25755648 | bytes 7130880 | tf_op jit(solution)/shard_map/rhtp,rphe->rhte/dot_general | solution.py:77
  52.6 0.2 copy.139
  52.9 0.2 fusion.5
  53.1 14.9 %all-reduce.1 = (bf16[3,16,4,64]{3,2,1,0:T(4,128)(2,1)S(1)}, bf16[3,16,4]{2,1,0:T(8,128)(2,1)S(1)}) all-reduce(bf16[3,16,4,64]{3,2,1,0:T(4,128)(2,1)S(1)} %fusion.5, bf16[3,16,4]{2,1,0:T(8,128)(2,1)S(1)} %get-tuple-element.42), channel_id=1, replica_groups=mesh['seq'=4,'tp'=32] {'seq'}, use_global_device_ids=true, to_apply=%region_3.4 | all-reduce | flops 12480 | bytes 49920 | tf_op jit(solution)/shard_map/psum | solution.py:93
  68.3 0.5 multiply_reduce_fusion
  68.9 26.4 %all_gather.15 = bf16[96,4,1024]{2,1,0:T(4,128)(2,1)S(1)} all-gather(bf16[3,4,1024]{2,1,0:T(4,128)(2,1)S(1)} %multiply_convert_fusion), channel_id=1, replica_groups=mesh['seq'=4,'tp'=32] {'tp'}, dimensions={0}, use_global_device_ids=true | all-gather | bytes 811008 | tf_op jit(solution)/shard_map/all_gather | solution.py:127
  95.3 23.6 %all-gather.1 = s32[32,4,16]{2,1,0:T(4,128)S(1)} all-gather(s32[1,4,16]{2,1,0:T(4,128)S(1)} %bitcast.39), channel_id=2, replica_groups=mesh['seq'=4,'tp'=32] {'tp'}, dimensions={0}, use_global_device_ids=true | all-gather | bytes 8448 | tf_op jit(solution)/shard_map/all_gather | solution.py:13
  119.0 0.3 select_reduce_fusion.1
  119.3 23.6 %all_gather.14 = s32[96,4,4]{2,1,0:T(4,128)S(1)} all-gather(s32[3,4,4]{2,1,0:T(4,128)S(1)} %copy.143), channel_id=1, replica_groups=mesh['seq'=4,'tp'=32] {'tp'}, dimensions={0}, use_global_device_ids=true | all-gather | bytes 6336 | tf_op jit(solution)/shard_map/all_gather | solution.py:124
  142.9 0.2 fusion.60
  143.2 0.4 fusion.9
  143.9 0.5 convolution_convert_fusion.1
  144.5 1.5 fusion.62
  145.9 2.0 fusion.7
  148.0 1.4 fusion.2
  149.4 1.5 copy.155
  151.0 0.6 dynamic-slice
  152.2 101.1 %all-reduce.4.cloned.1.call-done = bf16[96,4,1024]{2,1,0:T(4,128)(2,1)} async-done(((bf16[96,4,1024]{2,1,0:T(4,128)(2,1)}), bf16[96,4,1024]{2,1,0:T(4,128)(2,1)}) %all-reduce.4.cloned.1.call-update) | async-done | bytes 786448
  253.3 0.7 constant_dynamic-slice_fusion
  254.1 0.7 copy.156
  254.8 1.2 reshape.105
  256.0 0.6 dynamic-slice_convert_fusion
  256.6 19.6 %reduce-scatter.4.cloned.1.call-done = bf16[256,12]{1,0:T(8,128)(2,1)} async-done(((bf16[1024,12]{1,0:T(8,128)(2,1)}), bf16[256,12]{1,0:T(8,128)(2,1)}) %reduce-scatter.4.cloned.1.call-update) | async-done | bytes 6160
  276.3 1.0 reshape.106
  277.4 0.6 add_convert_fusion
  (58 shorter events, 2.3 us)
Async XLA Ops:
  7.2 61.1 %copy-start = (bf16[1024,1024]{1,0:T(8,128)(2,1)S(1)}, bf16[1024,1024]{1,0:T(8,128)(2,1)}, u32[]{:S(2)}) copy-start(bf16[1024,1024]{1,0:T(8,128)(2,1)} %param.23) | copy-start | bytes 6291460
  7.2 246.2 %all-reduce.4.cloned.1.call-start = ((), (), s32[]{:S(2)}) async-start(), calls=%async_computation.2 | async-start | bytes 1572864
  8.2 8.7 %copy-start.3 = (bf16[3,4,1024]{2,1,0:T(4,128)(2,1)S(1)}, bf16[3,4,1024]{2,1,0:T(4,128)(2,1)}, u32[]{:S(2)}) copy-start(bf16[3,4,1024]{2,1,0:T(4,128)(2,1)} %param.18) | copy-start | bytes 73732
  8.2 9.3 %copy-start.6 = (s32[3]{0:T(128)S(1)}, s32[3]{0:T(128)}, u32[]{:S(2)}) copy-start(s32[3]{0:T(128)} %param.22) | copy-start | bytes 40
  48.0 4.8 %copy-start.4 = (bf16[3,4,1024]{2,1,0:T(4,128)(2,1)S(1)}, bf16[3,4,1024]{2,1,0:T(4,128)(2,1)}, u32[]{:S(2)}) copy-start(bf16[3,4,1024]{2,1,0:T(4,128)(2,1)} %param.19) | copy-start | bytes 73732
  48.0 20.3 %copy-start.2 = (bf16[3,4,1024]{2,1,0:T(4,128)(2,1)S(1)}, bf16[3,4,1024]{2,1,0:T(4,128)(2,1)}, u32[]{:S(2)}) copy-start(bf16[3,4,1024]{2,1,0:T(4,128)(2,1)} %param.16) | copy-start | bytes 73732
  48.0 20.8 %copy-start.5 = (f32[1024]{0:T(1024)S(1)}, f32[1024]{0:T(1024)}, u32[]{:S(2)}) copy-start(f32[1024]{0:T(1024)} %param.24) | copy-start | bytes 12292
  48.0 47.3 %copy-start.1 = (s32[3,4,2]{1,2,0:T(2,128)S(1)}, s32[3,4,2]{1,2,0:T(2,128)}, u32[]{:S(2)}) copy-start(s32[3,4,2]{1,2,0:T(2,128)} %param.26) | copy-start | bytes 292
  48.0 95.2 %copy-start.7 = (bf16[1024,16]{0,1:T(8,128)(2,1)S(1)}, bf16[1024,16]{0,1:T(8,128)(2,1)}, u32[]{:S(2)}) copy-start(bf16[1024,16]{0,1:T(8,128)(2,1)} %param.25) | copy-start | bytes 98308
  68.8 82.2 %copy-start.8 = (u32[128]{0:T(128)S(1)}, u32[128]{0:T(128)}, u32[]{:S(2)}) copy-start(u32[128]{0:T(128)} %constant.85) | copy-start | bytes 1540
  150.9 125.3 %reduce-scatter.4.cloned.1.call-start = ((), (), s32[]{:S(2)}) async-start(), calls=%async_computation.1 | async-start | bytes 327680
Sparse Core Ops, SparseCore 0:
  151.1 102.2 all-reduce.3
  256.1 20.0 reduce-scatter.3
where the time goes:
time: 286 us; the launch traced here: 285 us
  waiting for transfers between devices  121 us (42%)
  blocking collectives  106 us (37%)
  local copies, waits for them, and re-layouts  26.3 us (9%)
  matrix products  15.1 us (5%)
  between operations  15 us (5%)
    unnamed x4, waiting for transfers between devices  121 us
    all_gather x1, blocking collectives, body(): all_normed = lax.all_gather(normed, 'tp', axis=0, tiled=True)  26.4 us
    all_gather x1, blocking collectives, entering(): gathered = lax.all_gather(part, axis)  23.6 us
    all_gather x1, blocking collectives, body(): all_routing = lax.all_gather(routing, 'tp', axis=0, tiled=True)  23.6 us
    unnamed x28, local copies, waits for them, and re-layouts  21.9 us
    pmax x1, blocking collectives, body(): overall = lax.pmax(local_max, 'seq')  17.1 us
    psum x1, blocking collectives, body(): lax.psum((gathered_values * factors[..., None]).astype(jnp.bfloat16), 'seq')  14.9 us
  transfers between devices with their start and end apart: 2, of which 2 were waited for; matrix products, arithmetic and copies ran while one was open for 0% of the time, Pallas kernels for 0%

commit v1 on v0

--- a/solution.py
+++ b/solution.py
@@ -6,6 +6,7 @@
 HEADS = 16
 masked_score = -1e30
 norm_epsilon = 1e-06
+handle_threads = lambda my_tile: jnp.sum(lax.all_gather(my_tile, "seq"), axis=0)
 
 
 def entering(part, axis, combine, identity):
@@ -90,7 +91,7 @@
     factors = jnp.exp(local_max - overall)
     totals, gathered_values = (
         lax.psum((totals * factors).astype(jnp.bfloat16), "seq").astype(jnp.float32),
-        lax.psum((gathered_values * factors[..., None]).astype(jnp.bfloat16), "seq").astype(
+        handle_threads((gathered_values * factors[..., None]).astype(jnp.bfloat16)).astype(
             jnp.float32
         ),
     )

time: 286 us -> 297 us (1.038)
  blocking collectives: 106 us -> 117 us
    all_gather x0 -> x1, blocking collectives: none -> 12.2 us  [lax.all_gather(my_tile, 'seq')]
where the time goes in v1:
time: 297 us; the launch traced here: 296 us
  waiting for transfers between devices  120 us (40%)
  blocking collectives  117 us (39%)
  local copies, waits for them, and re-layouts  26.3 us (9%)
  matrix products  15.1 us (5%)
  between operations  15 us (5%)
    unnamed x4, waiting for transfers between devices  120 us
    all_gather x1, blocking collectives, body(): all_normed = lax.all_gather(normed, 'tp', axis=0, tiled=True)  26.4 us
    all_gather x1, blocking collectives, entering(): gathered = lax.all_gather(part, axis)  23.6 us
    all_gather x1, blocking collectives, body(): all_routing = lax.all_gather(routing, 'tp', axis=0, tiled=True)  23.6 us
    unnamed x28, local copies, waits for them, and re-layouts  21.9 us
    pmax x1, blocking collectives, body(): overall = lax.pmax(local_max, 'seq')  17.1 us
    psum x1, blocking collectives, body(): lax.psum((totals * factors).astype(jnp.bfloat16), 'seq').astype(jnp.float32)  14.3 us
    all_gather x1, blocking collectives, lax.all_gather(my_tile, 'seq')  12.2 us
  transfers between devices with their start and end apart: 2, of which 2 were waited for; matrix products, arithmetic and copies ran while one was open for 0% of the time, Pallas kernels for 0%

profile of v1, /device:TPU:0, one launch (start us, length us, event | category | flops | bytes accessed | tf_op | source)
XLA Modules:
  0.0 295.8 jit_solution(14295587785396430981)
XLA Ops:
  7.2 1.0 reshape.92
  8.2 8.7 %copy.161 = bf16[3,1024,1024]{1,2,0:T(8,128)(2,1)} copy(bf16[3,1024,1024]{2,1,0:T(8,128)(2,1)} %param.20) | data formatting | bytes 12582912 | tf_op args[4]
  17.0 0.2 fusion.30
  17.6 3.8 %fusion.62 = (f32[3,16,4]{2,1,0:T(8,128)S(1)}, f32[3,16,4,1024]{3,2,1,0:T(4,128)S(1)}) fusion(bf16[3,1024,16,64]{1,3,2,0:T(8,128)(2,1)} %bitcast.42, bf16[3,4,16,64]{3,2,1,0:T(8,128)(2,1)S(1)} %reshape.92, pred[3,1024]{1,0:T(4,128)(4,1)S(1)} %broadcast_compare_fusion), kind=kOutput, calls=%fused_computation.94 | convolution fusion | flops 25755456 | bytes 7106304 | tf_op jit(solution)/shard_map/rthe,rphe->rhtp/dot_general | solution.py:62
  21.5 17.1 %pmax.7 = f32[3,16,4]{2,1,0:T(8,128)S(1)} all-reduce(f32[3,16,4]{2,1,0:T(8,128)S(1)} %max.9), channel_id=1, replica_groups=mesh['seq'=4,'tp'=32] {'seq'}, use_global_device_ids=true, to_apply=%region_2.3 | all-reduce | flops 192 | bytes 1536 | tf_op jit(solution)/shard_map/pmax | solution.py:90
  38.6 0.5 fusion.12
  39.3 8.6 %copy.167 = bf16[3,1024,1024]{1,2,0:T(8,128)(2,1)} copy(bf16[3,1024,1024]{2,1,0:T(8,128)(2,1)} %param.21) | data formatting | bytes 12582912 | tf_op args[5]
  48.0 4.6 %fusion.14 = f32[3,16,4,64]{3,2,1,0:T(4,128)S(1)} fusion(bf16[3,1024,16,64]{1,3,2,0:T(8,128)(2,1)} %bitcast.43, f32[3,16,4,1024]{3,2,1,0:T(4,128)S(1)} %get-tuple-element.47, f32[3,16,4]{2,1,0:T(8,128)S(1)} %max.9, pred[3,1024]{1,0:T(4,128)(4,1)S(1)} %broadcast_compare_fusion), kind=kOutput, calls=%fused_computation.22 | convolution fusion | flops 25755648 | bytes 7130880 | tf_op jit(solution)/shard_map/rhtp,rphe->rhte/dot_general | solution.py:78
  52.6 0.2 copy.169
  52.9 0.2 fusion.5
  53.1 12.2 %all-gather = bf16[12,16,4,64]{3,1,2,0:T(8,128)(2,1)S(1)} all-gather(bf16[3,16,4,64]{3,1,2,0:T(8,128)(2,1)S(1)} %copy.171), channel_id=2, replica_groups=mesh['seq'=4,'tp'=32] {'seq'}, dimensions={0}, use_global_device_ids=true | all-gather | bytes 122880 | tf_op jit(solution)/shard_map/all_gather | solution.py:9
  65.5 14.3 %psum.7 = bf16[3,4,16]{1,2,0:T(8,128)(2,1)S(1)} all-reduce(bf16[3,4,16]{1,2,0:T(8,128)(2,1)S(1)} %get-tuple-element.40), channel_id=1, replica_groups=mesh['seq'=4,'tp'=32] {'seq'}, use_global_device_ids=true, to_apply=%region_6.7 | all-reduce | flops 192 | bytes 768 | tf_op jit(solution)/shard_map/psum | solution.py:93
  80.0 0.5 multiply_reduce_fusion
  80.6 26.4 %all_gather.23 = bf16[96,4,1024]{2,1,0:T(4,128)(2,1)S(1)} all-gather(bf16[3,4,1024]{2,1,0:T(4,128)(2,1)S(1)} %multiply_convert_fusion), channel_id=1, replica_groups=mesh['seq'=4,'tp'=32] {'tp'}, dimensions={0}, use_global_device_ids=true | all-gather | bytes 811008 | tf_op jit(solution)/shard_map/all_gather | solution.py:128
  107.1 23.6 %all-gather.2 = s32[32,4,16]{2,1,0:T(4,128)S(1)} all-gather(s32[1,4,16]{2,1,0:T(4,128)S(1)} %bitcast.47), channel_id=3, replica_groups=mesh['seq'=4,'tp'=32] {'tp'}, dimensions={0}, use_global_device_ids=true | all-gather | bytes 8448 | tf_op jit(solution)/shard_map/all_gather | solution.py:14
  130.7 0.3 select_reduce_fusion.1
  131.1 23.6 %all_gather.22 = s32[96,4,4]{2,1,0:T(4,128)S(1)} all-gather(s32[3,4,4]{2,1,0:T(4,128)S(1)} %copy.175), channel_id=1, replica_groups=mesh['seq'=4,'tp'=32] {'tp'}, dimensions={0}, use_global_device_ids=true | all-gather | bytes 6336 | tf_op jit(solution)/shard_map/all_gather | solution.py:125
  154.9 0.4 fusion.9
  155.6 0.5 convolution_convert_fusion.1
  156.2 1.5 fusion.63
  157.7 2.0 fusion.7
  159.7 1.4 fusion.2
  161.1 1.5 copy.187
  162.8 0.6 dynamic-slice
  164.0 100.3 %all-reduce.3.cloned.1.call-done = bf16[96,4,1024]{2,1,0:T(4,128)(2,1)} async-done(((bf16[96,4,1024]{2,1,0:T(4,128)(2,1)}), bf16[96,4,1024]{2,1,0:T(4,128)(2,1)}) %all-reduce.3.cloned.1.call-update) | async-done | bytes 786448
  264.3 0.7 constant_dynamic-slice_fusion
  265.0 0.7 copy.188
  265.8 1.2 reshape.106
  267.0 0.6 dynamic-slice_convert_fusion
  267.6 19.6 %reduce-scatter.4.cloned.1.call-done = bf16[256,12]{1,0:T(8,128)(2,1)} async-done(((bf16[1024,12]{1,0:T(8,128)(2,1)}), bf16[256,12]{1,0:T(8,128)(2,1)}) %reduce-scatter.4.cloned.1.call-update) | async-done | bytes 6160
  287.2 1.0 reshape.107
  288.4 0.6 add_convert_fusion
  (62 shorter events, 2.5 us)
Async XLA Ops:
  7.2 72.8 %copy-start = (bf16[1024,1024]{1,0:T(8,128)(2,1)S(1)}, bf16[1024,1024]{1,0:T(8,128)(2,1)}, u32[]{:S(2)}) copy-start(bf16[1024,1024]{1,0:T(8,128)(2,1)} %param.23) | copy-start | bytes 6291460
  7.2 257.1 %all-reduce.3.cloned.1.call-start = ((), (), s32[]{:S(2)}) async-start(), calls=%async_computation.2 | async-start | bytes 1572864
  8.2 8.7 %copy-start.3 = (bf16[3,4,1024]{2,1,0:T(4,128)(2,1)S(1)}, bf16[3,4,1024]{2,1,0:T(4,128)(2,1)}, u32[]{:S(2)}) copy-start(bf16[3,4,1024]{2,1,0:T(4,128)(2,1)} %param.18) | copy-start | bytes 73732
  8.2 9.3 %copy-start.6 = (s32[3]{0:T(128)S(1)}, s32[3]{0:T(128)}, u32[]{:S(2)}) copy-start(s32[3]{0:T(128)} %param.22) | copy-start | bytes 40
  48.0 4.8 %copy-start.4 = (bf16[3,4,1024]{2,1,0:T(4,128)(2,1)S(1)}, bf16[3,4,1024]{2,1,0:T(4,128)(2,1)}, u32[]{:S(2)}) copy-start(bf16[3,4,1024]{2,1,0:T(4,128)(2,1)} %param.19) | copy-start | bytes 73732
  48.0 32.0 %copy-start.2 = (bf16[3,4,1024]{2,1,0:T(4,128)(2,1)S(1)}, bf16[3,4,1024]{2,1,0:T(4,128)(2,1)}, u32[]{:S(2)}) copy-start(bf16[3,4,1024]{2,1,0:T(4,128)(2,1)} %param.16) | copy-start | bytes 73732
  48.0 32.6 %copy-start.5 = (f32[1024]{0:T(1024)S(1)}, f32[1024]{0:T(1024)}, u32[]{:S(2)}) copy-start(f32[1024]{0:T(1024)} %param.24) | copy-start | bytes 12292
  48.0 59.0 %copy-start.1 = (s32[3,4,2]{1,2,0:T(2,128)S(1)}, s32[3,4,2]{1,2,0:T(2,128)}, u32[]{:S(2)}) copy-start(s32[3,4,2]{1,2,0:T(2,128)} %param.26) | copy-start | bytes 292
  48.0 106.9 %copy-start.7 = (bf16[1024,16]{0,1:T(8,128)(2,1)S(1)}, bf16[1024,16]{0,1:T(8,128)(2,1)}, u32[]{:S(2)}) copy-start(bf16[1024,16]{0,1:T(8,128)(2,1)} %param.25) | copy-start | bytes 98308
  80.5 82.2 %copy-start.8 = (u32[128]{0:T(128)S(1)}, u32[128]{0:T(128)}, u32[]{:S(2)}) copy-start(u32[128]{0:T(128)} %constant.87) | copy-start | bytes 1540
  162.7 124.5 %reduce-scatter.4.cloned.1.call-start = ((), (), s32[]{:S(2)}) async-start(), calls=%async_computation.1 | async-start | bytes 327680
Sparse Core Ops, SparseCore 0:
  162.8 101.4 all-reduce.2
  267.1 20.0 reduce-scatter.3
